TPU v7x, 32 devices: a whole 2x2x4 slice. The times are simulated.
32 devices in a mesh: seq: 8 (over y, x, core), tensor: 4 (over z).
Axes of the slice: x: 2, y: 2, z: 4, core: 2. Of those that a mesh axis runs over, the one named last changes fastest.
Arguments:
- queries: bfloat16 [1024, 4096], P(('seq', 'tensor')), may hold values from -5 to 5
- keys: bfloat16 [1024, 1024], P(('seq', 'tensor')), may hold values from -5 to 5
- values: bfloat16 [1024, 1024], P(('seq', 'tensor')), may hold values from -5 to 5
- mamba_x: bfloat16 [1024, 8192], P(('seq', 'tensor')), may hold values from -5 to 5
- mamba_b: bfloat16 [1024, 1024], P(('seq', 'tensor')), may hold values from -5 to 5
- mamba_c: bfloat16 [1024, 1024], P(('seq', 'tensor')), may hold values from -5 to 5
- mamba_dt: bfloat16 [1024, 128], P(('seq', 'tensor')), may hold values from -4 to 4
- conv_x: bfloat16 [4, 8192], P(None, 'tensor'), may hold values from -3 to 3
- conv_b: bfloat16 [4, 1024], P(None, 'tensor'), may hold values from -3 to 3
- conv_c: bfloat16 [4, 1024], P(None, 'tensor'), may hold values from -3 to 3
- dt_bias: float32 [128], P('tensor'), may hold values from -1 to 1
- decay_rate: float32 [128], P('tensor'), may hold values from 0.0001 to 0.05
- skip_gain: float32 [128], P('tensor'), may hold values from 0.5 to 1.5
- norm_gain: float32 [8192], P('tensor'), may hold values from 0.5 to 1.5
- windows: int32 [32], replicated, may hold values from 160 to 640, as said below
- doc_lengths: int32 [3], replicated, may hold values from 1 to 768, 1024 in all
Outputs:
- attn_out: bfloat16 [1024, 4096], P('seq', 'tensor')
- mamba_out: bfloat16 [1024, 8192], P('seq', 'tensor')
- attn_checksum: float32 [4096], P('tensor')
- mamba_checksum: float32 [8192], P('tensor')
Inputs may be any that keep to these rules, and one draw needn't show every extreme that they name: `windows`: one of the 32 query heads has a window of exactly 640 tokens. `doc_lengths`: 3 lengths summing to 1024; the longest is exactly three quarters of 1024.
All inputs are finite; a program needn't handle non-finite values.
Results may differ from a plain program's by a relative error of at most 0.007.
Values may be sent and summed in bfloat16 or wider, within the bound.
No kernel may reach another device: no remote copies, remote signals or barrier semaphores. Data moves between devices by JAX's collectives and lax.ppermute only.
A program may use at most 192 MiB of HBM per device.

v0:
```python
import math
import jax
import jax.numpy as jnp
from jax import lax
from jax.sharding import PartitionSpec as P

HEAD_SIZE = 128
MP = 64
MN = 128
KC = 4
NEG_LARGE = -1e30
EPS_NORM = 1e-05


def shifted(block, axis, distance):
    devices = range(lax.axis_size(axis))
    route = [(i - distance, i) for i in devices if i - distance in devices]
    return lax.ppermute(block, axis, route)


def prefix(x, axis, combine, identity):
    length, here = (lax.axis_size(axis), lax.axis_index(axis))
    everything = jax.tree.map(
        lambda part, kind: lax.all_gather(part.astype(kind), axis), x, (jnp.bfloat16, jnp.bfloat16)
    )
    start = jax.tree.map(
        lambda part, zero: jnp.broadcast_to(jnp.asarray(zero, part.dtype), part.shape), x, identity
    )

    def turn(k, before):
        reached = k < here
        new = combine(
            before, jax.tree.map(lambda part, own: part[k].astype(own.dtype), everything, x)
        )
        return jax.tree.map(lambda a, b: jnp.where(reached, a, b), new, before)

    return lax.fori_loop(0, length, turn, start)


def doc_table(doc_lengths):
    return jnp.cumsum(doc_lengths) - doc_lengths


def doc_index(positions, doc_starts):
    return jnp.sum((positions[:, None] >= doc_starts[None, :]).astype(jnp.int32), axis=1) - 1


def allowed_mask(query_pos, key_pos, doc_starts, window_per_head):
    gap = query_pos[:, None] - key_pos[None, :]
    same_doc = doc_index(query_pos, doc_starts)[:, None] == doc_index(key_pos, doc_starts)[None, :]
    base_ok = (gap >= 0) & (key_pos[None, :] >= 0) & same_doc
    return base_ok[None, None] & (gap[None, None] < window_per_head[:, :, None, None])


def attend_piece(
    carry, piece, key_start, grouped_heads, query_pos, doc_starts, window_per_head, reach
):
    key_rows, value_rows = piece
    key_count = key_rows.shape[0]
    shared_heads = grouped_heads.shape[1]
    key_pos = jnp.arange(key_count, dtype=jnp.int32)

    def compute(state):
        old_max, old_total, old_accum = state
        keys_rank3 = key_rows.reshape(key_count, shared_heads, HEAD_SIZE)
        values_rank3 = value_rows.reshape(key_count, shared_heads, HEAD_SIZE)
        scores = jnp.einsum(
            "tgqd,sgd->gqts", grouped_heads, keys_rank3, preferred_element_type=jnp.float32
        ) * (1.0 / math.sqrt(HEAD_SIZE))
        allowed = allowed_mask(query_pos, key_pos, doc_starts, window_per_head)
        scores = jnp.where(allowed, scores, NEG_LARGE)
        new_max = jnp.maximum(old_max, jnp.max(scores, axis=-1))
        weights = jnp.where(allowed, jnp.exp(scores - new_max[..., None]), 0.0)
        new_total = jnp.sum(weights, axis=-1)
        product = jnp.einsum(
            "gqts,sgd->gqtd",
            weights.astype(jnp.bfloat16),
            values_rank3,
            preferred_element_type=jnp.float32,
        )
        return (new_max, new_total, product)

    touches = (key_start + key_count - 1 >= query_pos[0] - reach) & (key_start <= query_pos[-1])
    return lax.cond(touches, compute, lambda state: state, carry)


def causal_conv(extended, taps, positions, doc_starts):
    count = positions.shape[0]
    docs_out = doc_index(positions, doc_starts)
    ext_pos = positions[0] - (KC - 1) + jnp.arange(count + KC - 1, dtype=jnp.int32)
    docs_ext = doc_index(ext_pos, doc_starts)
    running = jnp.zeros((count, extended.shape[1]), jnp.float32)
    for tap_index in range(KC):
        offset = KC - 1 - tap_index
        valid = (docs_ext[offset : offset + count] == docs_out) & (
            ext_pos[offset : offset + count] >= 0
        )
        term = taps[tap_index].astype(jnp.float32)[None, :] * extended[
            offset : offset + count
        ].astype(jnp.float32)
        running = running + jnp.where(valid[:, None], term, 0.0)
    return jax.nn.silu(running).astype(jnp.bfloat16)


def stretch_terms(x_rows, b_rows, c_rows, dt_rows, positions, doc_starts, dt_bias, decay_rate):
    count = positions.shape[0]
    heads = x_rows.shape[1] // MP
    groups = b_rows.shape[1] // MN
    per_group = heads // groups
    docs = doc_index(positions, doc_starts)
    prior_doc = doc_index(positions[:1] - 1, doc_starts)[0]
    delta = jax.nn.softplus(dt_rows.astype(jnp.float32) + dt_bias[None, :])
    log_decay = -delta * decay_rate[None, :]
    running = jnp.cumsum(log_decay, axis=0)
    running_heads = running.T
    order = jnp.arange(count, dtype=jnp.int32)
    causal = order[:, None] >= order[None, :]
    same_doc = docs[:, None] == docs[None, :]
    gaps = running_heads[:, :, None] - running_heads[:, None, :]
    segment = jnp.where((causal & same_doc)[None], jnp.exp(jnp.minimum(gaps, 0.0)), 0.0)
    inputs3 = x_rows.reshape(count, heads, MP)
    b_groups = b_rows.reshape(count, groups, MN)
    c_groups = c_rows.reshape(count, groups, MN)
    cross = jnp.einsum("tgn,sgn->gts", c_groups, b_groups, preferred_element_type=jnp.float32)
    cross_heads = jnp.repeat(cross, per_group, axis=0)
    mixing = (segment * cross_heads * delta.T[:, None, :]).astype(jnp.bfloat16)
    intra = jnp.einsum("hts,shp->thp", mixing, inputs3, preferred_element_type=jnp.float32)
    last_doc = docs[count - 1]
    to_end = (
        jnp.where((docs == last_doc)[:, None], jnp.exp(running[count - 1][None, :] - running), 0.0)
        * delta
    )
    weighted = (inputs3.astype(jnp.float32) * to_end[:, :, None]).astype(jnp.bfloat16)
    b_heads = jnp.repeat(b_groups, per_group, axis=1)
    local_state = jnp.einsum("shp,shn->hpn", weighted, b_heads, preferred_element_type=jnp.float32)
    carry_factor = jnp.where(prior_doc == last_doc, jnp.exp(running[count - 1]), 0.0)
    inflow = jnp.where((docs == prior_doc)[:, None], jnp.exp(running), 0.0)
    c_heads = jnp.repeat(c_groups, per_group, axis=1)
    return (intra, local_state, carry_factor, inflow, c_heads)


def stretch_finish(intra, incoming, inflow, c_heads, x_rows, skip_gain, norm_gain):
    count = x_rows.shape[0]
    heads = x_rows.shape[1] // MP
    incoming_bf = incoming.astype(jnp.bfloat16)
    entering = (
        jnp.einsum("thn,hpn->thp", c_heads, incoming_bf, preferred_element_type=jnp.float32)
        * inflow[:, :, None]
    )
    inputs3 = x_rows.reshape(count, heads, MP).astype(jnp.float32)
    mixed = intra + entering + skip_gain[None, :, None] * inputs3
    mean_square = jnp.mean(mixed * mixed, axis=-1, keepdims=True)
    normed = mixed * lax.rsqrt(mean_square + EPS_NORM) * norm_gain.reshape(heads, MP)[None]
    return normed.reshape(count, heads * MP).astype(jnp.bfloat16)


def combine_states(earlier, later):
    return (earlier[0] * later[0], later[0][:, None, None] * earlier[1] + later[1])


def local(
    queries,
    keys,
    values,
    mamba_x,
    mamba_b,
    mamba_c,
    mamba_dt,
    conv_x,
    conv_b,
    conv_c,
    dt_bias,
    decay_rate,
    skip_gain,
    norm_gain,
    windows,
    doc_lengths,
):
    served = (
        lax.all_to_all(queries, "tensor", split_axis=1, concat_axis=0, tiled=True),
        lax.all_to_all(keys, "tensor", split_axis=1, concat_axis=0, tiled=True),
        lax.all_to_all(values, "tensor", split_axis=1, concat_axis=0, tiled=True),
        lax.all_to_all(mamba_x, "tensor", split_axis=1, concat_axis=0, tiled=True),
        lax.all_to_all(mamba_b, "tensor", split_axis=1, concat_axis=0, tiled=True),
        lax.all_to_all(mamba_c, "tensor", split_axis=1, concat_axis=0, tiled=True),
        lax.all_to_all(mamba_dt, "tensor", split_axis=1, concat_axis=0, tiled=True),
    )
    query_rows, key_rows, value_rows, x_rows, b_rows, c_rows, dt_rows = served
    row_count = query_rows.shape[0]
    shard_start = lax.axis_index("seq") * row_count
    positions = shard_start + jnp.arange(row_count, dtype=jnp.int32)
    doc_starts = doc_table(doc_lengths)
    query_heads = query_rows.shape[1] // HEAD_SIZE
    shared_heads = key_rows.shape[1] // HEAD_SIZE
    group_width = query_heads // shared_heads
    window_per_head = lax.dynamic_slice_in_dim(
        windows, lax.axis_index("tensor") * query_heads, query_heads
    ).reshape(shared_heads, group_width)
    reach = jnp.max(window_per_head)
    grouped_heads = query_rows.reshape(row_count, shared_heads, group_width, HEAD_SIZE)
    initial = (
        jnp.full((shared_heads, group_width, row_count), NEG_LARGE, jnp.float32),
        jnp.zeros((shared_heads, group_width, row_count), jnp.float32),
        jnp.zeros((shared_heads, group_width, row_count, HEAD_SIZE), jnp.float32),
    )
    final = attend_piece(
        initial,
        (
            lax.all_gather(key_rows, "seq", axis=0, tiled=True),
            lax.all_gather(value_rows, "seq", axis=0, tiled=True),
        ),
        jnp.int32(0),
        grouped_heads,
        positions,
        doc_starts,
        window_per_head,
        reach,
    )
    final_max, totals, accum = final
    attention = (
        (accum / totals[..., None])
        .transpose(2, 0, 1, 3)
        .reshape(row_count, query_heads * HEAD_SIZE)
        .astype(jnp.bfloat16)
    )
    edge = row_count - (KC - 1)
    tails = shifted((x_rows[edge:], b_rows[edge:], c_rows[edge:]), "seq", 1)
    conv_x_out = causal_conv(
        jnp.concatenate([tails[0], x_rows], axis=0), conv_x, positions, doc_starts
    )
    conv_b_out = causal_conv(
        jnp.concatenate([tails[1], b_rows], axis=0), conv_b, positions, doc_starts
    )
    conv_c_out = causal_conv(
        jnp.concatenate([tails[2], c_rows], axis=0), conv_c, positions, doc_starts
    )
    intra, local_state, carry_factor, inflow, c_heads = stretch_terms(
        conv_x_out, conv_b_out, conv_c_out, dt_rows, positions, doc_starts, dt_bias, decay_rate
    )
    incoming = prefix(
        (carry_factor, local_state),
        "seq",
        combine_states,
        (jnp.ones_like(carry_factor), jnp.zeros_like(local_state)),
    )
    mamba_out = stretch_finish(
        intra, incoming[1], inflow, c_heads, conv_x_out, skip_gain, norm_gain
    )
    sums = lax.psum(
        (
            jnp.sum(attention.astype(jnp.float32), axis=0),
            jnp.sum(mamba_out.astype(jnp.float32), axis=0),
        ),
        "seq",
    )
    return (attention, mamba_out, sums[0], sums[1])


def solution(mesh):
    placed = (
        P(("seq", "tensor"), None),
        P(("seq", "tensor"), None),
        P(("seq", "tensor"), None),
        P(("seq", "tensor"), None),
        P(("seq", "tensor"), None),
        P(("seq", "tensor"), None),
        P(("seq", "tensor"), None),
        P(None, "tensor"),
        P(None, "tensor"),
        P(None, "tensor"),
        P("tensor"),
        P("tensor"),
        P("tensor"),
        P("tensor"),
        P(),
        P(),
    )
    return jax.shard_map(
        local,
        mesh=mesh,
        in_specs=placed,
        out_specs=(P("seq", "tensor"), P("seq", "tensor"), P("tensor"), P("tensor")),
        check_vma=False,
    )
```

profile of v0, /device:TPU:0, one launch (start us, length us, event | category | flops | bytes accessed | tf_op | source)
XLA Modules:
  0.0 185.0 jit_solution(2254786012537562026)
XLA Ops:
  7.2 0.8 all_to_all.107
  8.7 6.3 %all-to-all-start.4 = ((bf16[4,2,512]{2,1,0:T(2,128)(2,1)}), bf16[4,2,512]{2,1,0:T(2,128)(2,1)S(1)}, u32[]{:S(2)}, u32[]{:S(2)}) async-start(bf16[4,2,512]{2,1,0:T(2,128)(2,1)} %reshape.408), calls=%async_computation.4 | async-start | bytes 16384 | tf_op jit(solution)/shard_map/all_to_all | solution.py:186
  17.0 0.8 reduce-window.9
  17.8 1.3 fusion.30
  19.2 0.9 slice_convert_fusion.3
  20.1 0.8 slice_convert_fusion.7
  21.0 1.5 copy.168
  22.5 5.1 %all-to-all-start.6 = ((bf16[32,4,256]{2,0,1:T(8,128)(2,1)}), bf16[32,4,256]{2,0,1:T(8,128)(2,1)S(1)}, u32[]{:S(2)}, u32[]{:S(2)}) async-start(bf16[32,4,256]{2,0,1:T(8,128)(2,1)} %bitcast.129), calls=%async_computation.6 | async-start | bytes 131072 | tf_op jit(solution)/shard_map/all_to_all | solution.py:184
  28.1 1.9 %copy.166 = bf16[4,4,8,2048]{3,2,0,1:T(8,128)(2,1)} copy(bf16[4,4,8,2048]{3,2,1,0:T(8,128)(2,1)} %bitcast.155) | data formatting | bytes 1048576 | tf_op jit(solution)/shard_map/all_to_all | solution.py:183
  30.6 2.7 %all-to-all-done.6 = bf16[32,4,256]{2,0,1:T(8,128)(2,1)S(1)} async-done(((bf16[32,4,256]{2,0,1:T(8,128)(2,1)}), bf16[32,4,256]{2,0,1:T(8,128)(2,1)S(1)}, u32[]{:S(2)}, u32[]{:S(2)}) %all-to-all-start.6) | async-done | bytes 65568 | tf_op jit(solution)/shard_map/all_to_all | solution.py:184
  33.3 3.6 %all-to-all-start.3 = ((bf16[32,4,2048]{2,0,1:T(8,128)(2,1)}), bf16[32,4,2048]{2,0,1:T(8,128)(2,1)S(1)}, u32[]{:S(2)}, u32[]{:S(2)}) async-start(bf16[32,4,2048]{2,0,1:T(8,128)(2,1)} %bitcast.127), calls=%async_computation.3 | async-start | bytes 1048576 | tf_op jit(solution)/shard_map/all_to_all | solution.py:183
  39.4 1.3 collective-permute-start.2
  40.7 0.8 select_multiply_fusion
  41.5 8.2 %all-to-all-done.3 = bf16[32,4,2048]{2,0,1:T(8,128)(2,1)S(1)} async-done(((bf16[32,4,2048]{2,0,1:T(8,128)(2,1)}), bf16[32,4,2048]{2,0,1:T(8,128)(2,1)S(1)}, u32[]{:S(2)}, u32[]{:S(2)}) %all-to-all-start.3) | async-done | bytes 524320 | tf_op jit(solution)/shard_map/all_to_all | solution.py:183
  49.7 1.3 collective-permute-start
  51.8 1.0 multiply_convert_fusion.1
  53.3 1.2 convolution_convert_fusion
  55.2 3.3 %all-to-all-start.5 = ((bf16[32,4,256]{2,0,1:T(8,128)(2,1)}), bf16[32,4,256]{2,0,1:T(8,128)(2,1)S(1)}, u32[]{:S(2)}, u32[]{:S(2)}) async-start(bf16[32,4,256]{2,0,1:T(8,128)(2,1)} %bitcast.130), calls=%async_computation.5 | async-start | bytes 131072 | tf_op jit(solution)/shard_map/all_to_all | solution.py:185
  61.3 2.9 %all-to-all-done.5 = bf16[32,4,256]{2,0,1:T(8,128)(2,1)S(1)} async-done(((bf16[32,4,256]{2,0,1:T(8,128)(2,1)}), bf16[32,4,256]{2,0,1:T(8,128)(2,1)S(1)}, u32[]{:S(2)}, u32[]{:S(2)}) %all-to-all-start.5) | async-done | bytes 65568 | tf_op jit(solution)/shard_map/all_to_all | solution.py:185
  64.2 3.3 %all-to-all-start = ((bf16[32,4,256]{2,0,1:T(8,128)(2,1)}), bf16[32,4,256]{2,0,1:T(8,128)(2,1)S(1)}, u32[]{:S(2)}, u32[]{:S(2)}) async-start(bf16[32,4,256]{2,0,1:T(8,128)(2,1)} %bitcast.132), calls=%async_computation | async-start | bytes 131072 | tf_op jit(solution)/shard_map/all_to_all | solution.py:181
  67.5 1.3 fusion.31
  70.8 12.8 %all-gather.1 = bf16[8,1,32]{2,1,0:T(2,128)(2,1)S(1)} all-gather(bf16[1,1,32]{2,1,0:T(2,128)(2,1)S(1)} %get-tuple-element.210), channel_id=1, replica_groups=mesh['seq'=8,'tensor'=4] {'seq'}, dimensions={0}, use_global_device_ids=true | all-gather | bytes 576 | tf_op jit(solution)/shard_map/all_gather | solution.py:24
  85.0 2.2 %collective-permute-start.1 = (bf16[3,256]{1,0:T(4,128)(2,1)S(1)}, bf16[3,256]{1,0:T(4,128)(2,1)S(1)}, u32[]{:S(2)}, u32[]{:S(2)}) collective-permute-start(bf16[3,256]{1,0:T(4,128)(2,1)S(1)} %slice.170), channel_id=1, source_target_pairs={{0,4},{4,8},{8,12},{12,16},{16,20},{20,24},{24,28},{1,5},{5,9},{9,... | collective-permute-start | bytes 4616 | tf_op jit(solution)/shard_map/ppermute | solution.py:18
  87.2 5.1 %all-to-all-start.2 = ((bf16[32,4,256]{2,0,1:T(8,128)(2,1)}), bf16[32,4,256]{2,0,1:T(8,128)(2,1)S(1)}, u32[]{:S(2)}, u32[]{:S(2)}) async-start(bf16[32,4,256]{2,0,1:T(8,128)(2,1)} %bitcast.131), calls=%async_computation.2 | async-start | bytes 131072 | tf_op jit(solution)/shard_map/all_to_all | solution.py:182
  92.3 9.3 %all_gather.16 = bf16[1024,256]{1,0:T(8,128)(2,1)S(1)} all-gather(bf16[128,256]{1,0:T(8,128)(2,1)S(1)} %bitcast.162), channel_id=1, replica_groups=mesh['seq'=8,'tensor'=4] {'seq'}, dimensions={0}, use_global_device_ids=true | all-gather | bytes 589824 | tf_op jit(solution)/shard_map/all_gather | solution.py:209
  101.6 4.7 %all-to-all-start.1 = ((bf16[32,4,1024]{2,0,1:T(8,128)(2,1)}), bf16[32,4,1024]{2,0,1:T(8,128)(2,1)S(1)}, u32[]{:S(2)}, u32[]{:S(2)}) async-start(bf16[32,4,1024]{2,0,1:T(8,128)(2,1)} %bitcast.128), calls=%async_computation.1 | async-start | bytes 524288 | tf_op jit(solution)/shard_map/all_to_all | solution.py:180
  106.3 9.7 %all_gather.17 = bf16[1024,256]{1,0:T(8,128)(2,1)S(1)} all-gather(bf16[128,256]{1,0:T(8,128)(2,1)S(1)} %bitcast.163), channel_id=1, replica_groups=mesh['seq'=8,'tensor'=4] {'seq'}, dimensions={0}, use_global_device_ids=true | all-gather | bytes 589824 | tf_op jit(solution)/shard_map/all_gather | solution.py:210
  117.3 1.6 fusion.13
  118.9 13.4 %conditional.1 = (f32[2,4,128]{2,1,0:T(4,128)S(1)}, f32[2,4,128,128]{3,2,1,0:T(8,128)S(1)}) conditional(s32[]{:T(128)} %convert_element_type.180, () %tuple.30, (s32[128]{0:T(128)S(1)}, s32[1024]{0:T(1024)S(1)}, s32[1024]{0:T(1024)S(1)}, s32[3]{0:T(128)S(1)}, s32[1024]{0:T(1024)S(1)}, /*index=5*/s32[8]{0:T(128)}, bf16[1024,256]{1,0:T(8,128)(2,1)S(1)}, ...), branch_computations={%region_2.3_spmd, %region_3.8_spmd} | conditional | flops 557590656 | bytes 36501220 | solution.py:84
  119.1 0.9 compare_and_fusion.1
  120.9 0.9 reshape.367
  122.0 4.1 %fusion = (f32[2,4,128]{2,1,0:T(4,128)S(1)}, f32[2,1024,128,4]{2,1,3,0:T(8,128)}) fusion(s32[2,4]{1,0:T(2,128)S(1)} %lt.30, s32[128,1024]{0,1:T(8,128)S(1)} %broadcast_subtract_fusion, pred[128,1024]{0,1:T(8,128)(4,1)S(1)} %compare_and_fusion.1, bf16[128,2,4,128]{3,2,1,0:T(4,128)(2,1)S(1)} %reshape.368, bf16[1024,2,128,1]{2,1,0,3:T(2,128)(2,1)} %bitcast.156), kind=kOutput, calls=%fused_computation.3 | convolution fusion | flops 273677312 | bytes 5640224 | tf_op jit(solution)/shard_map/cond/branch_1_fun/tgqd,sgd->gqts/dot_general | solution.py:67
  126.3 4.3 %fusion.1 = f32[2,4,128,128]{3,2,1,0:T(8,128)S(1)} fusion(f32[2,1024,128,4]{2,1,3,0:T(8,128)} %get-tuple-element.206, f32[2,4,128]{2,1,0:T(4,128)S(1)} %broadcast_maximum_fusion, s32[2,4]{1,0:T(2,128)S(1)} %lt.30, s32[128,1024]{0,1:T(8,128)S(1)} %broadcast_subtract_fusion, pred[128,1024]{0,1:T(8,128)(4,1)S(1)} %compare_and_fusion.1, ...), kind=kOutput, calls=%fused_computation.4 | convolution fusion | flops 275775488 | bytes 5902368 | tf_op jit(solution)/shard_map/cond/branch_1_fun/gqts,sgd->gqtd/dot_general | solution.py:75
  130.6 1.6 fusion.3
  132.7 0.9 convert_element_type.183
  133.5 2.0 %convolution_bitcast_fusion.1 = f32[128,32,64]{0,2,1:T(8,128)S(1)} fusion(bf16[128,32,64]{0,2,1:T(8,128)(2,1)S(1)} %bitcast.140, bf16[32,128,128]{2,1,0:T(8,128)(2,1)} %fusion.13), kind=kOutput, calls=%fused_computation.32 | convolution fusion | flops 67108864 | bytes 2621440 | tf_op jit(solution)/shard_map/hts,shp->thp/dot_general | solution.py:127
  135.6 16.0 %while.14 = (s32[]{:T(128)}, f32[32,64,128]{2,1,0:T(8,128)S(1)}, s32[]{:T(128)}, bf16[8,32]{1,0:T(8,128)(2,1)}, bf16[8,32,64,128]{3,2,1,0:T(8,128)(2,1)}, /*index=5*/s32[]{:T(128)}, s32[]{:T(128)}) while((s32[]{:T(128)}, f32[32,64,128]{2,1,0:T(8,128)S(1)}, s32[]{:T(128)}, bf16[8,32]{1,0:T(8,128)(2,1)}, ...), condition=%wide.region_13.14_spmd.clone, body=%wide.region_12.13_spmd.clone.sunk | while | flops 1310756 | bytes 2621865 | solution.py:37
  136.3 1.3 fusion.41
  138.3 1.3 fusion.41
  140.3 1.3 fusion.41
  142.3 1.3 fusion.41
  144.3 1.3 fusion.41
  146.4 1.3 fusion.41
  148.4 1.3 fusion.41
  150.4 1.3 fusion.41
  151.9 0.9 multiply_reduce_fusion
  153.6 1.0 copy.131
  154.6 23.6 %all-reduce = (f32[1024]{0:T(1024)}, f32[2048]{0:T(1024)}) all-reduce(f32[1024]{0:T(1024)S(1)} %bitcast.175, f32[2048]{0:T(1024)S(1)} %reduce_sum.112), channel_id=1, replica_groups=mesh['seq'=8,'tensor'=4] {'seq'}, use_global_device_ids=true, to_apply=%region_16.17 | all-reduce | flops 3072 | bytes 24576 | tf_op jit(solution)/shard_map/psum | solution.py:249
  (99 shorter events, 19.6 us)
Async XLA Ops:
  8.7 13.8 %all-to-all-start.4 = ((bf16[4,2,512]{2,1,0:T(2,128)(2,1)}), bf16[4,2,512]{2,1,0:T(2,128)(2,1)S(1)}, u32[]{:S(2)}, u32[]{:S(2)}) async-start(bf16[4,2,512]{2,1,0:T(2,128)(2,1)} %reshape.408), calls=%async_computation.4 | async-start | bytes 16384 | tf_op jit(solution)/shard_map/all_to_all | solution.py:186
  22.5 10.8 %all-to-all-start.6 = ((bf16[32,4,256]{2,0,1:T(8,128)(2,1)}), bf16[32,4,256]{2,0,1:T(8,128)(2,1)S(1)}, u32[]{:S(2)}, u32[]{:S(2)}) async-start(bf16[32,4,256]{2,0,1:T(8,128)(2,1)} %bitcast.129), calls=%async_computation.6 | async-start | bytes 131072 | tf_op jit(solution)/shard_map/all_to_all | solution.py:184
  30.0 24.6 %copy-start.5 = (bf16[32,1024]{1,0:T(8,128)(2,1)S(1)}, bf16[32,1024]{1,0:T(8,128)(2,1)}, u32[]{:S(2)}) copy-start(bf16[32,1024]{1,0:T(8,128)(2,1)} %param.25) | copy-start | bytes 196612
  33.3 25.3 %copy-start.9 = (bf16[4,256]{1,0:T(4,128)(2,1)S(1)}, bf16[4,256]{1,0:T(4,128)(2,1)}, u32[]{:S(2)}) copy-start(bf16[4,256]{1,0:T(4,128)(2,1)} %param.29) | copy-start | bytes 6148
  33.3 25.3 %copy-start.8 = (f32[2048]{0:T(1024)S(1)}, f32[2048]{0:T(1024)}, u32[]{:S(2)}) copy-start(f32[2048]{0:T(1024)} %param.33) | copy-start | bytes 24580
  33.3 26.0 %copy-start.6 = (bf16[32,1024]{1,0:T(8,128)(2,1)S(1)}, bf16[32,1024]{1,0:T(8,128)(2,1)}, u32[]{:S(2)}) copy-start(bf16[32,1024]{1,0:T(8,128)(2,1)} %param.21) | copy-start | bytes 196612
  33.3 26.6 %copy-start.7 = (bf16[32,1024]{1,0:T(8,128)(2,1)S(1)}, bf16[32,1024]{1,0:T(8,128)(2,1)}, u32[]{:S(2)}) copy-start(bf16[32,1024]{1,0:T(8,128)(2,1)} %param.22) | copy-start | bytes 196612
  33.3 27.2 %copy-start.2 = (bf16[32,4096]{1,0:T(8,128)(2,1)S(1)}, bf16[32,4096]{1,0:T(8,128)(2,1)}, u32[]{:S(2)}) copy-start(bf16[32,4096]{1,0:T(8,128)(2,1)} %param.20) | copy-start | bytes 786436
  33.3 16.4 %all-to-all-start.3 = ((bf16[32,4,2048]{2,0,1:T(8,128)(2,1)}), bf16[32,4,2048]{2,0,1:T(8,128)(2,1)S(1)}, u32[]{:S(2)}, u32[]{:S(2)}) async-start(bf16[32,4,2048]{2,0,1:T(8,128)(2,1)} %bitcast.127), calls=%async_computation.3 | async-start | bytes 1048576 | tf_op jit(solution)/shard_map/all_to_all | solution.py:183
  36.9 30.6 %copy-start.11 = (s32[32]{0:T(128)S(1)}, s32[32]{0:T(128)}, u32[]{:S(2)}) copy-start(s32[32]{0:T(128)} %param.34) | copy-start | bytes 388
  37.0 98.6 %all-gather.4.cloned.1.call-start = ((), (), s32[]{:S(2)}) async-start(), calls=%async_computation.7 | async-start | bytes 4718592 | tf_op jit(solution)/shard_map/all_gather | solution.py:24
  39.4 11.6 %collective-permute-start.2 = (bf16[3,256]{1,0:T(4,128)(2,1)S(1)}, bf16[3,256]{1,0:T(4,128)(2,1)S(1)}, u32[]{:S(2)}, u32[]{:S(2)}) collective-permute-start(bf16[3,256]{1,0:T(4,128)(2,1)S(1)} %slice.175), channel_id=1, source_target_pairs={{0,4},{4,8},{8,12},{12,16},{16,20},{20,24},{24,28},{1,5},{5,9},{9,... | collective-permute-start | bytes 4616 | tf_op jit(solution)/shard_map/ppermute | solution.py:18
  49.7 2.1 %collective-permute-start = (bf16[3,2048]{1,0:T(4,128)(2,1)S(1)}, bf16[3,2048]{1,0:T(4,128)(2,1)S(1)}, u32[]{:S(2)}, u32[]{:S(2)}) collective-permute-start(bf16[3,2048]{1,0:T(4,128)(2,1)S(1)} %slice.165), channel_id=1, source_target_pairs={{0,4},{4,8},{8,12},{12,16},{16,20},{20,24},{24,28},{1,5},{5,9},{9,... | collective-permute-start | bytes 36872 | tf_op jit(solution)/shard_map/ppermute | solution.py:18
  55.2 9.0 %all-to-all-start.5 = ((bf16[32,4,256]{2,0,1:T(8,128)(2,1)}), bf16[32,4,256]{2,0,1:T(8,128)(2,1)S(1)}, u32[]{:S(2)}, u32[]{:S(2)}) async-start(bf16[32,4,256]{2,0,1:T(8,128)(2,1)} %bitcast.130), calls=%async_computation.5 | async-start | bytes 131072 | tf_op jit(solution)/shard_map/all_to_all | solution.py:185
  64.2 23.0 %all-to-all-start = ((bf16[32,4,256]{2,0,1:T(8,128)(2,1)}), bf16[32,4,256]{2,0,1:T(8,128)(2,1)S(1)}, u32[]{:S(2)}, u32[]{:S(2)}) async-start(bf16[32,4,256]{2,0,1:T(8,128)(2,1)} %bitcast.132), calls=%async_computation | async-start | bytes 131072 | tf_op jit(solution)/shard_map/all_to_all | solution.py:181
  85.0 31.1 %collective-permute-start.1 = (bf16[3,256]{1,0:T(4,128)(2,1)S(1)}, bf16[3,256]{1,0:T(4,128)(2,1)S(1)}, u32[]{:S(2)}, u32[]{:S(2)}) collective-permute-start(bf16[3,256]{1,0:T(4,128)(2,1)S(1)} %slice.170), channel_id=1, source_target_pairs={{0,4},{4,8},{8,12},{12,16},{16,20},{20,24},{24,28},{1,5},{5,9},{9,... | collective-permute-start | bytes 4616 | tf_op jit(solution)/shard_map/ppermute | solution.py:18
  87.2 14.4 %all-to-all-start.2 = ((bf16[32,4,256]{2,0,1:T(8,128)(2,1)}), bf16[32,4,256]{2,0,1:T(8,128)(2,1)S(1)}, u32[]{:S(2)}, u32[]{:S(2)}) async-start(bf16[32,4,256]{2,0,1:T(8,128)(2,1)} %bitcast.131), calls=%async_computation.2 | async-start | bytes 131072 | tf_op jit(solution)/shard_map/all_to_all | solution.py:182
  101.6 17.3 %all-to-all-start.1 = ((bf16[32,4,1024]{2,0,1:T(8,128)(2,1)}), bf16[32,4,1024]{2,0,1:T(8,128)(2,1)S(1)}, u32[]{:S(2)}, u32[]{:S(2)}) async-start(bf16[32,4,1024]{2,0,1:T(8,128)(2,1)} %bitcast.128), calls=%async_computation.1 | async-start | bytes 524288 | tf_op jit(solution)/shard_map/all_to_all | solution.py:180
  126.3 4.4 %copy-start = (f32[2,1024,128,4]{2,1,3,0:T(8,128)S(1)}, f32[2,1024,128,4]{2,1,3,0:T(8,128)}, u32[]{:S(2)}) copy-start(f32[2,1024,128,4]{2,1,3,0:T(8,128)} %get-tuple-element.206) | copy-start | bytes 12582916 | tf_op jit(solution)/shard_map/cond
  135.6 16.1 %copy-start.1 = (bf16[128,2,128]{2,0,1:T(8,128)(2,1)S(1)}, bf16[128,2,128]{2,0,1:T(8,128)(2,1)}, u32[]{:S(2)}) copy-start(bf16[128,2,128]{2,0,1:T(8,128)(2,1)} %copy.129) | copy-start | bytes 196612
  135.6 16.3 %copy-start.3 = (f32[128,32]{0,1:T(8,128)S(1)}, f32[128,32]{0,1:T(8,128)}, u32[]{:S(2)}) copy-start(f32[128,32]{0,1:T(8,128)} %copy.130) | copy-start | bytes 49156
  135.6 16.3 %copy-start.10 = (f32[32]{0:T(128)S(1)}, f32[32]{0:T(128)}, u32[]{:S(2)}) copy-start(f32[32]{0:T(128)} %param.32) | copy-start | bytes 388
  151.7 1.2 copy-start.4
Sparse Core Ops, SparseCore 0:
  54.7 38.6 all-gather.3
where the time goes:
time: 187 us; the launch traced here: 185 us
  blocking collectives  55.4 us (30%)
  starting transfers between devices  36.3 us (19%)
  other arithmetic  30.3 us (16%)
  between operations  19 us (10%)
  local copies, waits for them, and re-layouts  16.8 us (9%)
  waiting for transfers between devices  14.2 us (8%)
  matrix products  12.8 us (7%)
    psum x1, blocking collectives, local(): lax.psum((jnp.sum(attention.astype(jnp.float32), axis=0), jnp.sum(mamba_o...  23.6 us
    all_gather x1, blocking collectives, prefix(): lax.all_gather(part.astype(kind), axis)  12.8 us
    select_n x8, other arithmetic, turn(): return jax.tree.map(lambda a, b: jnp.where(reached, a, b), new, before)  10.4 us
    all_gather x1, blocking collectives, local(): lax.all_gather(value_rows, 'seq', axis=0, tiled=True)  9.74 us
    all_gather x1, blocking collectives, local(): lax.all_gather(key_rows, 'seq', axis=0, tiled=True)  9.29 us
    all_to_all x1, waiting for transfers between devices, local(): lax.all_to_all(mamba_x, 'tensor', split_axis=1, concat_axis=0, tiled=True)  8.17 us
    all_to_all x1, starting transfers between devices, local(): lax.all_to_all(mamba_dt, 'tensor', split_axis=1, concat_axis=0, tiled=True)  6.35 us
    convert_element_type x8, other arithmetic, turn(): part[k].astype(own.dtype)  5.54 us
  transfers between devices with their start and end apart: 11, of which 4 were waited for; matrix products, arithmetic and copies ran while one was open for 20% of the time, Pallas kernels for 0%

commit v1 on v0

--- a/solution.py
+++ b/solution.py
@@ -180,7 +180,12 @@
         lax.all_to_all(queries, "tensor", split_axis=1, concat_axis=0, tiled=True),
         lax.all_to_all(keys, "tensor", split_axis=1, concat_axis=0, tiled=True),
         lax.all_to_all(values, "tensor", split_axis=1, concat_axis=0, tiled=True),
-        lax.all_to_all(mamba_x, "tensor", split_axis=1, concat_axis=0, tiled=True),
+        jnp.concatenate(
+            lax.all_to_all(
+                jnp.stack(jnp.split(mamba_x, lax.axis_size("tensor"), axis=1)), "tensor", 0, 0
+            ),
+            axis=0,
+        ),
         lax.all_to_all(mamba_b, "tensor", split_axis=1, concat_axis=0, tiled=True),
         lax.all_to_all(mamba_c, "tensor", split_axis=1, concat_axis=0, tiled=True),
         lax.all_to_all(mamba_dt, "tensor", split_axis=1, concat_axis=0, tiled=True),

time: 187 us -> 195 us (1.043)
  blocking collectives: 55.4 us -> 60.1 us
  waiting for transfers between devices: 14.2 us -> 16.6 us
  other arithmetic: 30.3 us -> 32.4 us
    all_gather x1, blocking collectives: 12.8 us -> 17.5 us  [prefix(): lax.all_gather(part.astype(kind), axis)]
  transfers between devices with their start and end apart: 11 -> 11, of which waited for: 4 -> 4; matrix products, arithmetic and copies ran while one was open for 20% -> 19% of each run, Pallas kernels for 0% -> 0%
where the time goes in v1:
time: 195 us; the launch traced here: 194 us
  blocking collectives  60.1 us (31%)
  starting transfers between devices  36.2 us (19%)
  other arithmetic  32.4 us (17%)
  between operations  19 us (10%)
  waiting for transfers between devices  16.6 us (9%)
  local copies, waits for them, and re-layouts  16.2 us (8%)
  matrix products  12.8 us (7%)
    psum x1, blocking collectives, local(): lax.psum((jnp.sum(attention.astype(jnp.float32), axis=0), jnp.sum(mamba_o...  23.6 us
    all_gather x1, blocking collectives, prefix(): lax.all_gather(part.astype(kind), axis)  17.5 us
    select_n x8, other arithmetic, turn(): return jax.tree.map(lambda a, b: jnp.where(reached, a, b), new, before)  10.4 us
    all_gather x1, blocking collectives, local(): lax.all_gather(value_rows, 'seq', axis=0, tiled=True)  9.74 us
    all_gather x1, blocking collectives, local(): lax.all_gather(key_rows, 'seq', axis=0, tiled=True)  9.29 us
    all_to_all x1, waiting for transfers between devices, local(): lax.all_to_all(jnp.stack(jnp.split(mamba_x, lax.axis_size('tensor'), axis...  8.13 us
    all_to_all x1, starting transfers between devices, local(): lax.all_to_all(mamba_dt, 'tensor', split_axis=1, concat_axis=0, tiled=True)  6.35 us
    convert_element_type x8, other arithmetic, turn(): part[k].astype(own.dtype)  5.54 us
  transfers between devices with their start and end apart: 11, of which 4 were waited for; matrix products, arithmetic and copies ran while one was open for 19% of the time, Pallas kernels for 0%

profile of v1, /device:TPU:0, one launch (start us, length us, event | category | flops | bytes accessed | tf_op | source)
XLA Modules:
  0.0 193.6 jit_solution(13610859817464591192)
XLA Ops:
  8.7 6.3 %all-to-all-start.4 = ((bf16[4,2,512]{2,1,0:T(2,128)(2,1)}), bf16[4,2,512]{2,1,0:T(2,128)(2,1)S(1)}, u32[]{:S(2)}, u32[]{:S(2)}) async-start(bf16[4,2,512]{2,1,0:T(2,128)(2,1)} %reshape.409), calls=%async_computation.4 | async-start | bytes 16384 | tf_op jit(solution)/shard_map/all_to_all | solution.py:191
  16.9 0.8 reduce-window.9
  17.7 1.4 fusion.30
  19.2 1.1 slice_bitcast_fusion.3
  20.3 0.9 slice_convert_fusion.3
  21.2 0.8 slice_convert_fusion.7
  22.0 0.9 pad_maximum_fusion.1
  23.0 1.5 copy.172
  24.5 5.1 %all-to-all-start.6 = ((bf16[32,4,256]{2,0,1:T(8,128)(2,1)}), bf16[32,4,256]{2,0,1:T(8,128)(2,1)S(1)}, u32[]{:S(2)}, u32[]{:S(2)}) async-start(bf16[32,4,256]{2,0,1:T(8,128)(2,1)} %bitcast.131), calls=%async_computation.6 | async-start | bytes 131072 | tf_op jit(solution)/shard_map/all_to_all | solution.py:189
  30.8 4.5 %all-to-all-done.6 = bf16[32,4,256]{2,0,1:T(8,128)(2,1)S(1)} async-done(((bf16[32,4,256]{2,0,1:T(8,128)(2,1)}), bf16[32,4,256]{2,0,1:T(8,128)(2,1)S(1)}, u32[]{:S(2)}, u32[]{:S(2)}) %all-to-all-start.6) | async-done | bytes 65568 | tf_op jit(solution)/shard_map/all_to_all | solution.py:189
  35.3 3.5 %all-to-all-start.3 = ((bf16[4,32,2048]{2,1,0:T(8,128)(2,1)}), bf16[4,32,2048]{2,1,0:T(8,128)(2,1)S(1)}, u32[]{:S(2)}, u32[]{:S(2)}) async-start(bf16[4,32,2048]{2,1,0:T(8,128)(2,1)} %pad_maximum_fusion.1), calls=%async_computation.3 | async-start | bytes 1048576 | tf_op jit(solution)/shard_map/all_to_all | solution.py:184
  41.2 1.3 collective-permute-start.2
  43.4 8.1 %all-to-all-done.3 = bf16[4,32,2048]{2,1,0:T(8,128)(2,1)S(1)} async-done(((bf16[4,32,2048]{2,1,0:T(8,128)(2,1)}), bf16[4,32,2048]{2,1,0:T(8,128)(2,1)S(1)}, u32[]{:S(2)}, u32[]{:S(2)}) %all-to-all-start.3) | async-done | bytes 524320 | tf_op jit(solution)/shard_map/all_to_all | solution.py:184
  52.0 1.3 collective-permute-start
  53.8 1.1 collective-permute-done
  54.8 2.2 %multiply_convert_fusion.1 = bf16[128,2048]{0,1:T(8,128)(2,1)S(1)} fusion(bf16[128,2048]{0,1:T(8,128)(2,1)S(1)} %copy.121, bf16[3,2048]{0,1:T(8,128)(2,1)S(1)} %collective-permute-done, f32[2048]{0:T(1024)S(1)} %bitcast.173, f32[2048]{0:T(1024)S(1)} %bitcast.174, f32[2048]{0:T(1024)S(1)} %bitcast.172, f32[2048]{0:T(1024)S(1)} %bitcast.171, ...), kind=kLoop, calls=%fused_computation.44 | loop fusion | flops 7602176 | bytes 1094144 | tf_op jit(solution)/shard_map/convert_element_type | solution.py:102
  57.3 1.2 convolution_convert_fusion
  59.1 3.3 %all-to-all-start.5 = ((bf16[32,4,256]{2,0,1:T(8,128)(2,1)}), bf16[32,4,256]{2,0,1:T(8,128)(2,1)S(1)}, u32[]{:S(2)}, u32[]{:S(2)}) async-start(bf16[32,4,256]{2,0,1:T(8,128)(2,1)} %bitcast.132), calls=%async_computation.5 | async-start | bytes 131072 | tf_op jit(solution)/shard_map/all_to_all | solution.py:190
  65.2 2.9 %all-to-all-done.5 = bf16[32,4,256]{2,0,1:T(8,128)(2,1)S(1)} async-done(((bf16[32,4,256]{2,0,1:T(8,128)(2,1)}), bf16[32,4,256]{2,0,1:T(8,128)(2,1)S(1)}, u32[]{:S(2)}, u32[]{:S(2)}) %all-to-all-start.5) | async-done | bytes 65568 | tf_op jit(solution)/shard_map/all_to_all | solution.py:190
  68.1 3.3 %all-to-all-start = ((bf16[32,4,256]{2,0,1:T(8,128)(2,1)}), bf16[32,4,256]{2,0,1:T(8,128)(2,1)S(1)}, u32[]{:S(2)}, u32[]{:S(2)}) async-start(bf16[32,4,256]{2,0,1:T(8,128)(2,1)} %bitcast.134), calls=%async_computation | async-start | bytes 131072 | tf_op jit(solution)/shard_map/all_to_all | solution.py:181
  71.4 1.2 fusion.31
  74.6 17.5 %all-gather.1 = bf16[8,1,32]{2,1,0:T(2,128)(2,1)S(1)} all-gather(bf16[1,1,32]{2,1,0:T(2,128)(2,1)S(1)} %get-tuple-element.214), channel_id=1, replica_groups=mesh['seq'=8,'tensor'=4] {'seq'}, dimensions={0}, use_global_device_ids=true | all-gather | bytes 576 | tf_op jit(solution)/shard_map/all_gather | solution.py:24
  93.6 2.2 %collective-permute-start.1 = (bf16[3,256]{1,0:T(4,128)(2,1)S(1)}, bf16[3,256]{1,0:T(4,128)(2,1)S(1)}, u32[]{:S(2)}, u32[]{:S(2)}) collective-permute-start(bf16[3,256]{1,0:T(4,128)(2,1)S(1)} %slice.170), channel_id=1, source_target_pairs={{0,4},{4,8},{8,12},{12,16},{16,20},{20,24},{24,28},{1,5},{5,9},{9,... | collective-permute-start | bytes 4616 | tf_op jit(solution)/shard_map/ppermute | solution.py:18
  95.8 5.1 %all-to-all-start.2 = ((bf16[32,4,256]{2,0,1:T(8,128)(2,1)}), bf16[32,4,256]{2,0,1:T(8,128)(2,1)S(1)}, u32[]{:S(2)}, u32[]{:S(2)}) async-start(bf16[32,4,256]{2,0,1:T(8,128)(2,1)} %bitcast.133), calls=%async_computation.2 | async-start | bytes 131072 | tf_op jit(solution)/shard_map/all_to_all | solution.py:182
  100.9 9.3 %all_gather.16 = bf16[1024,256]{1,0:T(8,128)(2,1)S(1)} all-gather(bf16[128,256]{1,0:T(8,128)(2,1)S(1)} %bitcast.162), channel_id=1, replica_groups=mesh['seq'=8,'tensor'=4] {'seq'}, dimensions={0}, use_global_device_ids=true | all-gather | bytes 589824 | tf_op jit(solution)/shard_map/all_gather | solution.py:214
  110.2 4.7 %all-to-all-start.1 = ((bf16[32,4,1024]{2,0,1:T(8,128)(2,1)}), bf16[32,4,1024]{2,0,1:T(8,128)(2,1)S(1)}, u32[]{:S(2)}, u32[]{:S(2)}) async-start(bf16[32,4,1024]{2,0,1:T(8,128)(2,1)} %bitcast.130), calls=%async_computation.1 | async-start | bytes 524288 | tf_op jit(solution)/shard_map/all_to_all | solution.py:180
  114.9 9.7 %all_gather.17 = bf16[1024,256]{1,0:T(8,128)(2,1)S(1)} all-gather(bf16[128,256]{1,0:T(8,128)(2,1)S(1)} %bitcast.163), channel_id=1, replica_groups=mesh['seq'=8,'tensor'=4] {'seq'}, dimensions={0}, use_global_device_ids=true | all-gather | bytes 589824 | tf_op jit(solution)/shard_map/all_gather | solution.py:215
  125.9 1.6 fusion.13
  127.5 13.3 %conditional.1 = (f32[2,4,128]{2,1,0:T(4,128)S(1)}, f32[2,4,128,128]{3,2,1,0:T(8,128)S(1)}) conditional(s32[]{:T(128)} %convert_element_type.180, () %tuple.30, (s32[128]{0:T(128)S(1)}, s32[1024]{0:T(1024)S(1)}, s32[1024]{0:T(1024)S(1)}, s32[3]{0:T(128)S(1)}, s32[1024]{0:T(1024)S(1)}, /*index=5*/s32[8]{0:T(128)}, bf16[1024,256]{1,0:T(8,128)(2,1)S(1)}, ...), branch_computations={%region_2.3_spmd, %region_3.8_spmd} | conditional | flops 557590656 | bytes 36501220 | solution.py:84
  127.7 0.9 compare_and_fusion.1
  129.5 0.9 reshape.366
  130.6 4.1 %fusion = (f32[2,4,128]{2,1,0:T(4,128)S(1)}, f32[2,1024,128,4]{2,1,3,0:T(8,128)}) fusion(s32[2,4]{1,0:T(2,128)S(1)} %lt.30, s32[128,1024]{0,1:T(8,128)S(1)} %broadcast_subtract_fusion, pred[128,1024]{0,1:T(8,128)(4,1)S(1)} %compare_and_fusion.1, bf16[128,2,4,128]{3,2,1,0:T(4,128)(2,1)S(1)} %reshape.367, bf16[1024,2,128,1]{2,1,0,3:T(2,128)(2,1)} %bitcast.156), kind=kOutput, calls=%fused_computation.3 | convolution fusion | flops 273677312 | bytes 5640224 | tf_op jit(solution)/shard_map/cond/branch_1_fun/tgqd,sgd->gqts/dot_general | solution.py:67
  134.8 4.3 %fusion.1 = f32[2,4,128,128]{3,2,1,0:T(8,128)S(1)} fusion(f32[2,1024,128,4]{2,1,3,0:T(8,128)} %get-tuple-element.206, f32[2,4,128]{2,1,0:T(4,128)S(1)} %broadcast_maximum_fusion, s32[2,4]{1,0:T(2,128)S(1)} %lt.30, s32[128,1024]{0,1:T(8,128)S(1)} %broadcast_subtract_fusion, pred[128,1024]{0,1:T(8,128)(4,1)S(1)} %compare_and_fusion.1, ...), kind=kOutput, calls=%fused_computation.4 | convolution fusion | flops 275775488 | bytes 5902368 | tf_op jit(solution)/shard_map/cond/branch_1_fun/gqts,sgd->gqtd/dot_general | solution.py:75
  139.2 1.6 fusion.3
  141.2 0.9 convert_element_type.183
  142.1 2.0 %convolution_bitcast_fusion.1 = f32[128,32,64]{0,2,1:T(8,128)S(1)} fusion(bf16[128,32,64]{0,2,1:T(8,128)(2,1)S(1)} %bitcast.142, bf16[32,128,128]{2,1,0:T(8,128)(2,1)} %fusion.13), kind=kOutput, calls=%fused_computation.32 | convolution fusion | flops 67108864 | bytes 2621440 | tf_op jit(solution)/shard_map/hts,shp->thp/dot_general | solution.py:127
  144.2 16.0 %while.14 = (s32[]{:T(128)}, f32[32,64,128]{2,1,0:T(8,128)S(1)}, s32[]{:T(128)}, bf16[8,32]{1,0:T(8,128)(2,1)}, bf16[8,32,64,128]{3,2,1,0:T(8,128)(2,1)}, /*index=5*/s32[]{:T(128)}, s32[]{:T(128)}) while((s32[]{:T(128)}, f32[32,64,128]{2,1,0:T(8,128)S(1)}, s32[]{:T(128)}, bf16[8,32]{1,0:T(8,128)(2,1)}, ...), condition=%wide.region_13.14_spmd.clone, body=%wide.region_12.13_spmd.clone.sunk | while | flops 1310756 | bytes 2621865 | solution.py:37
  144.9 1.3 fusion.41
  146.9 1.3 fusion.41
  148.9 1.3 fusion.41
  150.9 1.3 fusion.41
  152.9 1.3 fusion.41
  154.9 1.3 fusion.41
  156.9 1.3 fusion.41
  158.9 1.3 fusion.41
  160.5 0.9 multiply_reduce_fusion
  162.1 1.0 copy.138
  163.1 23.6 %all-reduce = (f32[1024]{0:T(1024)}, f32[2048]{0:T(1024)}) all-reduce(f32[1024]{0:T(1024)S(1)} %bitcast.175, f32[2048]{0:T(1024)S(1)} %reduce_sum.112), channel_id=1, replica_groups=mesh['seq'=8,'tensor'=4] {'seq'}, use_global_device_ids=true, to_apply=%region_16.17 | all-reduce | flops 3072 | bytes 24576 | tf_op jit(solution)/shard_map/psum | solution.py:254
  (100 shorter events, 20.9 us)
Async XLA Ops:
  8.7 15.8 %all-to-all-start.4 = ((bf16[4,2,512]{2,1,0:T(2,128)(2,1)}), bf16[4,2,512]{2,1,0:T(2,128)(2,1)S(1)}, u32[]{:S(2)}, u32[]{:S(2)}) async-start(bf16[4,2,512]{2,1,0:T(2,128)(2,1)} %reshape.409), calls=%async_computation.4 | async-start | bytes 16384 | tf_op jit(solution)/shard_map/all_to_all | solution.py:191
  24.5 10.8 %all-to-all-start.6 = ((bf16[32,4,256]{2,0,1:T(8,128)(2,1)}), bf16[32,4,256]{2,0,1:T(8,128)(2,1)S(1)}, u32[]{:S(2)}, u32[]{:S(2)}) async-start(bf16[32,4,256]{2,0,1:T(8,128)(2,1)} %bitcast.131), calls=%async_computation.6 | async-start | bytes 131072 | tf_op jit(solution)/shard_map/all_to_all | solution.py:189
  35.3 16.2 %all-to-all-start.3 = ((bf16[4,32,2048]{2,1,0:T(8,128)(2,1)}), bf16[4,32,2048]{2,1,0:T(8,128)(2,1)S(1)}, u32[]{:S(2)}, u32[]{:S(2)}) async-start(bf16[4,32,2048]{2,1,0:T(8,128)(2,1)} %pad_maximum_fusion.1), calls=%async_computation.3 | async-start | bytes 1048576 | tf_op jit(solution)/shard_map/all_to_all | solution.py:184
  38.8 105.3 %all-gather.4.cloned.1.call-start = ((), (), s32[]{:S(2)}) async-start(), calls=%async_computation.7 | async-start | bytes 4718592 | tf_op jit(solution)/shard_map/all_gather | solution.py:24
  41.0 17.5 %copy-start.5 = (bf16[32,1024]{1,0:T(8,128)(2,1)S(1)}, bf16[32,1024]{1,0:T(8,128)(2,1)}, u32[]{:S(2)}) copy-start(bf16[32,1024]{1,0:T(8,128)(2,1)} %param.25) | copy-start | bytes 196612
  41.2 12.1 %collective-permute-start.2 = (bf16[3,256]{1,0:T(4,128)(2,1)S(1)}, bf16[3,256]{1,0:T(4,128)(2,1)S(1)}, u32[]{:S(2)}, u32[]{:S(2)}) collective-permute-start(bf16[3,256]{1,0:T(4,128)(2,1)S(1)} %slice.175), channel_id=1, source_target_pairs={{0,4},{4,8},{8,12},{12,16},{16,20},{20,24},{24,28},{1,5},{5,9},{9,... | collective-permute-start | bytes 4616 | tf_op jit(solution)/shard_map/ppermute | solution.py:18
  43.3 19.2 %copy-start.9 = (bf16[4,256]{1,0:T(4,128)(2,1)S(1)}, bf16[4,256]{1,0:T(4,128)(2,1)}, u32[]{:S(2)}) copy-start(bf16[4,256]{1,0:T(4,128)(2,1)} %param.29) | copy-start | bytes 6148
  43.3 19.2 %copy-start.8 = (f32[2048]{0:T(1024)S(1)}, f32[2048]{0:T(1024)}, u32[]{:S(2)}) copy-start(f32[2048]{0:T(1024)} %param.33) | copy-start | bytes 24580
  43.3 19.9 %copy-start.6 = (bf16[32,1024]{1,0:T(8,128)(2,1)S(1)}, bf16[32,1024]{1,0:T(8,128)(2,1)}, u32[]{:S(2)}) copy-start(bf16[32,1024]{1,0:T(8,128)(2,1)} %param.21) | copy-start | bytes 196612
  43.4 20.5 %copy-start.7 = (bf16[32,1024]{1,0:T(8,128)(2,1)S(1)}, bf16[32,1024]{1,0:T(8,128)(2,1)}, u32[]{:S(2)}) copy-start(bf16[32,1024]{1,0:T(8,128)(2,1)} %param.22) | copy-start | bytes 196612
  51.5 13.0 %copy-start.2 = (bf16[32,4096]{1,0:T(8,128)(2,1)S(1)}, bf16[32,4096]{1,0:T(8,128)(2,1)}, u32[]{:S(2)}) copy-start(bf16[32,4096]{1,0:T(8,128)(2,1)} %param.20) | copy-start | bytes 786436
  51.8 19.6 %copy-start.11 = (s32[32]{0:T(128)S(1)}, s32[32]{0:T(128)}, u32[]{:S(2)}) copy-start(s32[32]{0:T(128)} %param.34) | copy-start | bytes 388
  52.0 2.8 %collective-permute-start = (bf16[3,2048]{0,1:T(8,128)(2,1)S(1)}, bf16[3,2048]{0,1:T(8,128)(2,1)S(1)}, u32[]{:S(2)}, u32[]{:S(2)}) collective-permute-start(bf16[3,2048]{0,1:T(8,128)(2,1)S(1)} %slice.165), channel_id=1, source_target_pairs={{0,4},{4,8},{8,12},{12,16},{16,20},{20,24},{24,28},{1,5},{5,9},{9,... | collective-permute-start | bytes 36872 | tf_op jit(solution)/shard_map/ppermute | solution.py:18
  59.1 9.0 %all-to-all-start.5 = ((bf16[32,4,256]{2,0,1:T(8,128)(2,1)}), bf16[32,4,256]{2,0,1:T(8,128)(2,1)S(1)}, u32[]{:S(2)}, u32[]{:S(2)}) async-start(bf16[32,4,256]{2,0,1:T(8,128)(2,1)} %bitcast.132), calls=%async_computation.5 | async-start | bytes 131072 | tf_op jit(solution)/shard_map/all_to_all | solution.py:190
  68.1 27.7 %all-to-all-start = ((bf16[32,4,256]{2,0,1:T(8,128)(2,1)}), bf16[32,4,256]{2,0,1:T(8,128)(2,1)S(1)}, u32[]{:S(2)}, u32[]{:S(2)}) async-start(bf16[32,4,256]{2,0,1:T(8,128)(2,1)} %bitcast.134), calls=%async_computation | async-start | bytes 131072 | tf_op jit(solution)/shard_map/all_to_all | solution.py:181
  93.6 31.1 %collective-permute-start.1 = (bf16[3,256]{1,0:T(4,128)(2,1)S(1)}, bf16[3,256]{1,0:T(4,128)(2,1)S(1)}, u32[]{:S(2)}, u32[]{:S(2)}) collective-permute-start(bf16[3,256]{1,0:T(4,128)(2,1)S(1)} %slice.170), channel_id=1, source_target_pairs={{0,4},{4,8},{8,12},{12,16},{16,20},{20,24},{24,28},{1,5},{5,9},{9,... | collective-permute-start | bytes 4616 | tf_op jit(solution)/shard_map/ppermute | solution.py:18
  95.8 14.4 %all-to-all-start.2 = ((bf16[32,4,256]{2,0,1:T(8,128)(2,1)}), bf16[32,4,256]{2,0,1:T(8,128)(2,1)S(1)}, u32[]{:S(2)}, u32[]{:S(2)}) async-start(bf16[32,4,256]{2,0,1:T(8,128)(2,1)} %bitcast.133), calls=%async_computation.2 | async-start | bytes 131072 | tf_op jit(solution)/shard_map/all_to_all | solution.py:182
  110.2 17.3 %all-to-all-start.1 = ((bf16[32,4,1024]{2,0,1:T(8,128)(2,1)}), bf16[32,4,1024]{2,0,1:T(8,128)(2,1)S(1)}, u32[]{:S(2)}, u32[]{:S(2)}) async-start(bf16[32,4,1024]{2,0,1:T(8,128)(2,1)} %bitcast.130), calls=%async_computation.1 | async-start | bytes 524288 | tf_op jit(solution)/shard_map/all_to_all | solution.py:180
  134.8 4.4 %copy-start = (f32[2,1024,128,4]{2,1,3,0:T(8,128)S(1)}, f32[2,1024,128,4]{2,1,3,0:T(8,128)}, u32[]{:S(2)}) copy-start(f32[2,1024,128,4]{2,1,3,0:T(8,128)} %get-tuple-element.206) | copy-start | bytes 12582916 | tf_op jit(solution)/shard_map/cond
  144.1 16.1 %copy-start.1 = (bf16[128,2,128]{2,0,1:T(8,128)(2,1)S(1)}, bf16[128,2,128]{2,0,1:T(8,128)(2,1)}, u32[]{:S(2)}) copy-start(bf16[128,2,128]{2,0,1:T(8,128)(2,1)} %copy.136) | copy-start | bytes 196612
  144.2 16.3 %copy-start.3 = (f32[128,32]{0,1:T(8,128)S(1)}, f32[128,32]{0,1:T(8,128)}, u32[]{:S(2)}) copy-start(f32[128,32]{0,1:T(8,128)} %copy.137) | copy-start | bytes 49156
  144.2 16.3 %copy-start.10 = (f32[32]{0:T(128)S(1)}, f32[32]{0:T(128)}, u32[]{:S(2)}) copy-start(f32[32]{0:T(128)} %param.32) | copy-start | bytes 388
  160.2 1.2 copy-start.4
Sparse Core Ops, SparseCore 0:
  58.6 43.3 all-gather.3
